TPU v7x, 32 devices: a whole 2x2x4 slice. The times are simulated.
32 devices in a mesh: dp: 2 (over y), seq: 4 (over z), chan: 4 (over x, core).
Axes of the slice: x: 2, y: 2, z: 4, core: 2. Of those that a mesh axis runs over, the one named last changes fastest.
Arguments:
- tokens: bfloat16 [16384, 1024], P(('dp', 'seq'), 'chan'), may hold values from -6 to 6
- gain_one: bfloat16 [1024], P('chan'), may hold values from 0.25 to 1.75
- in_weight: bfloat16 [1024, 3, 1024], P(None, None, 'chan'), may hold values from -0.1875 to 0.1875
- conv_weight: bfloat16 [3, 1024], P(None, 'chan'), may hold values from -3 to 3
- out_weight: bfloat16 [1024, 1024], P('chan'), may hold values from -0.1875 to 0.1875
- gain_two: bfloat16 [1024], replicated, may hold values from 0.25 to 1.75
- gate_up_weight: bfloat16 [1024, 2, 4608], P(None, None, 'chan'), may hold values from -0.1875 to 0.1875
- down_weight: bfloat16 [4608, 1024], P('chan'), may hold values from -0.09375 to 0.09375
- cotangent: bfloat16 [16384, 1024], P(('dp', 'seq'), 'chan'), may hold values from -6 to 6
Outputs:
- result: bfloat16 [16384, 1024], P(('dp', 'seq'), 'chan')
- grad_tokens: bfloat16 [16384, 1024], P(('dp', 'seq'), 'chan')
- grad_gain_one: float32 [1024], P('chan')
- grad_in_weight: float32 [1024, 3, 1024], P(None, None, 'chan')
- grad_conv_weight: float32 [3, 1024], P(None, 'chan')
- grad_out_weight: float32 [1024, 1024], P('chan')
- grad_gain_two: float32 [1024], P('chan')
- grad_gate_up: float32 [1024, 2, 4608], P(None, None, 'chan')
- grad_down: float32 [4608, 1024], P('chan')
All inputs are finite; a program needn't handle non-finite values.
Results may differ from a plain program's by a relative error of at most 0.018.
Values may be sent and summed in bfloat16 or wider, within the bound.
No kernel may reach another device: no remote copies, remote signals or barrier semaphores. Data moves between devices by JAX's collectives and lax.ppermute only.
A program may use at most 256 MiB of HBM per device.

v0:
```python
import jax
import jax.numpy as jnp
from jax import lax
from jax.sharding import PartitionSpec as P

epsilon = 1e-05


def shifted(value, axis, by):
    length = lax.axis_size(axis)
    pairs = [(i, i + by) for i in range(length) if 0 <= i + by < length]
    return lax.ppermute(value, axis, pairs)


def shards(
    tokens,
    gain_one,
    in_weight,
    conv_weight,
    out_weight,
    gain_two,
    gate_up_weight,
    down_weight,
    cotangent,
):
    width = in_weight.shape[0]
    local_width = in_weight.shape[2]
    hidden_local = gate_up_weight.shape[2]
    count = tokens.shape[0]
    offset = lax.axis_index("chan") * local_width
    in_flat = in_weight.reshape(width, 3 * local_width)
    gu_flat = gate_up_weight.reshape(width, 2 * hidden_local)
    kernel = conv_weight.astype(jnp.float32)
    gain_second = gain_two.astype(jnp.float32)
    tokens_local = tokens.astype(jnp.float32)
    tokens_full, gain_full = (
        lax.all_gather(tokens, "chan", axis=1, tiled=True),
        lax.all_gather(gain_one, "chan", axis=0, tiled=True),
    )
    x_float = tokens_full.astype(jnp.float32)
    inv_one = lax.rsqrt(jnp.mean(x_float * x_float, axis=-1, keepdims=True) + epsilon)
    normed_one = (x_float * inv_one * gain_full.astype(jnp.float32)).astype(jnp.bfloat16)
    projected = jnp.dot(normed_one, in_flat, preferred_element_type=jnp.float32)
    gate_b = projected[:, :local_width]
    gate_c = projected[:, local_width : 2 * local_width]
    values = projected[:, 2 * local_width :]
    product = gate_b * values
    state = shifted(product[count - 2 :], "seq", 1)
    extended = jnp.concatenate([state, product], axis=0)
    conv_out = (
        kernel[0] * extended[0:count]
        + kernel[1] * extended[1 : count + 1]
        + kernel[2] * extended[2 : count + 2]
    )
    mixed = (gate_c * conv_out).astype(jnp.bfloat16)
    mix_partial = jnp.dot(mixed, out_weight, preferred_element_type=jnp.float32)
    resid = x_float + lax.psum(mix_partial, "chan")
    inv_two = lax.rsqrt(jnp.mean(resid * resid, axis=-1, keepdims=True) + epsilon)
    scaled_two = resid * inv_two
    normed_two = (scaled_two * gain_second).astype(jnp.bfloat16)
    resid_local = lax.dynamic_slice_in_dim(resid, offset, local_width, 1)
    gate_up = jnp.dot(normed_two, gu_flat, preferred_element_type=jnp.float32)
    gate_pre = gate_up[:, :hidden_local]
    up_pre = gate_up[:, hidden_local:]
    sigma = jax.nn.sigmoid(gate_pre)
    hidden = (gate_pre * sigma * up_pre).astype(jnp.bfloat16)
    ffn_local = lax.psum_scatter(
        jnp.dot(hidden, down_weight, preferred_element_type=jnp.float32).astype(jnp.bfloat16),
        "chan",
        scatter_dimension=1,
        tiled=True,
    ).astype(jnp.float32)
    result = (resid_local + ffn_local).astype(jnp.bfloat16)
    cot_full = lax.all_gather(cotangent, "chan", axis=1, tiled=True)
    d_hidden = jnp.dot(cot_full, down_weight.T, preferred_element_type=jnp.float32)
    grad_down = jnp.dot(hidden.T, cot_full, preferred_element_type=jnp.float32)
    d_gate = d_hidden * up_pre * sigma * (1.0 + gate_pre * (1.0 - sigma))
    d_up = d_hidden * gate_pre * sigma
    d_gate_up = jnp.concatenate([d_gate, d_up], axis=1).astype(jnp.bfloat16)
    grad_gate_up = jnp.dot(normed_two.T, d_gate_up, preferred_element_type=jnp.float32).reshape(
        width, 2, hidden_local
    )
    norm_partial = jnp.dot(d_gate_up, gu_flat.T, preferred_element_type=jnp.float32)
    d_norm_two = lax.psum(norm_partial, "chan")
    grad_gain_two = lax.dynamic_slice_in_dim(
        jnp.sum(d_norm_two * scaled_two, axis=0), offset, local_width, 0
    )
    pulled_two = d_norm_two * gain_second
    d_resid = cot_full.astype(jnp.float32) + inv_two * (
        pulled_two - scaled_two * jnp.mean(pulled_two * scaled_two, axis=-1, keepdims=True)
    )
    d_out = d_resid.astype(jnp.bfloat16)
    d_resid_local = lax.dynamic_slice_in_dim(d_resid, offset, local_width, 1)
    d_mixed = jnp.dot(d_out, out_weight.T, preferred_element_type=jnp.float32)
    grad_out = jnp.dot(mixed.T, d_out, preferred_element_type=jnp.float32)
    d_gate_c = d_mixed * conv_out
    d_conv = d_mixed * gate_c
    next_grad = shifted(d_conv[0:2], "seq", -1)
    grad_ext = jnp.concatenate([d_conv, next_grad], axis=0)
    d_product = (
        kernel[2] * grad_ext[0:count]
        + kernel[1] * grad_ext[1 : count + 1]
        + kernel[0] * grad_ext[2 : count + 2]
    )
    grad_conv = jnp.stack(
        [
            jnp.sum(d_conv * extended[shift_index : shift_index + count], axis=0)
            for shift_index in range(3)
        ]
    )
    d_project = jnp.concatenate([d_product * values, d_gate_c, d_product * gate_b], axis=1).astype(
        jnp.bfloat16
    )
    grad_in = jnp.dot(normed_one.T, d_project, preferred_element_type=jnp.float32).reshape(
        width, 3, local_width
    )
    d_norm_one = lax.psum_scatter(
        jnp.dot(d_project, in_flat.T, preferred_element_type=jnp.float32).astype(jnp.bfloat16),
        "chan",
        scatter_dimension=1,
        tiled=True,
    ).astype(jnp.float32)
    scaled_one = tokens_local * inv_one
    grad_gain_one = jnp.sum(d_norm_one * scaled_one, axis=0)
    pulled_one = d_norm_one * gain_one.astype(jnp.float32)
    inner_sum = lax.psum(jnp.sum(pulled_one * scaled_one, axis=-1, keepdims=True), "chan")
    grad_tokens = (
        d_resid_local + inv_one * (pulled_one - scaled_one * (inner_sum / width))
    ).astype(jnp.bfloat16)
    grad_gain_one, grad_in, grad_conv, grad_out, grad_gain_two, grad_gate_up, grad_down = (
        lax.psum(grad_gain_one.astype(jnp.bfloat16), ("dp", "seq")).astype(jnp.float32),
        lax.psum(grad_in.astype(jnp.bfloat16), ("dp", "seq")).astype(jnp.float32),
        lax.psum(grad_conv.astype(jnp.bfloat16), ("dp", "seq")).astype(jnp.float32),
        lax.psum(grad_out.astype(jnp.bfloat16), ("dp", "seq")).astype(jnp.float32),
        lax.psum(grad_gain_two.astype(jnp.bfloat16), ("dp", "seq")).astype(jnp.float32),
        lax.psum(grad_gate_up.astype(jnp.bfloat16), ("dp", "seq")).astype(jnp.float32),
        lax.psum(grad_down.astype(jnp.bfloat16), ("dp", "seq")).astype(jnp.float32),
    )
    return (
        result,
        grad_tokens,
        grad_gain_one,
        grad_in,
        grad_conv,
        grad_out,
        grad_gain_two,
        grad_gate_up,
        grad_down,
    )


def solution(mesh):
    placed = (
        P(("dp", "seq"), "chan"),
        P("chan"),
        P(None, None, "chan"),
        P(None, "chan"),
        P("chan", None),
        P(),
        P(None, None, "chan"),
        P("chan", None),
        P(("dp", "seq"), "chan"),
    )
    return jax.shard_map(
        shards,
        mesh=mesh,
        in_specs=placed,
        out_specs=(
            P(("dp", "seq"), "chan"),
            P(("dp", "seq"), "chan"),
            P("chan"),
            P(None, None, "chan"),
            P(None, "chan"),
            P("chan", None),
            P("chan"),
            P(None, None, "chan"),
            P("chan", None),
        ),
        check_vma=False,
    )
```

profile of v0, /device:TPU:0, one launch (start us, length us, event | category | flops | bytes accessed | tf_op | source)
XLA Modules:
  0.0 858.1 jit_solution(401732263966881372)
XLA Ops:
  8.0 2.6 copy.25
  10.6 6.0 all-gather
  16.6 30.7 %all-gather.4.cloned.1.call-done = bf16[2048,1024]{1,0:T(8,128)(2,1)} async-done(((bf16[2048,256]{1,0:T(8,128)(2,1)}), bf16[2048,1024]{1,0:T(8,128)(2,1)}) %all-gather.4.cloned.1.call-update) | async-done | bytes 4194320 | tf_op jit(solution)/shard_map/all_gather | solution.py:37
  47.3 3.2 fusion
  50.8 5.0 fusion.27
  56.1 3.5 collective-permute-start
  59.7 1.3 collective-permute-done
  61.0 2.0 multiply_convert_fusion.7
  63.0 1.0 copy-done.10
  64.0 4.7 fusion.36
  69.8 5.4 copy.30
  75.1 147.3 %all-reduce.6.cloned.1.call-done = f32[2048,1024]{1,0:T(8,128)} async-done(((f32[2048,1024]{1,0:T(8,128)}), f32[2048,1024]{1,0:T(8,128)}) %all-reduce.6.cloned.1.call-update) | async-done | bytes 8388624 | tf_op jit(solution)/shard_map/psum | solution.py:57
  222.5 5.7 multiply_reduce_fusion.2
  228.2 3.4 copy-done.3
  231.6 16.3 %fusion.33 = f32[2048,2304]{1,0:T(8,128)} fusion(bf16[1024,2304]{1,0:T(8,128)(2,1)} %bitcast.27, f32[2048,1024]{1,0:T(8,128)S(1)} %get-tuple-element.27, f32[1024]{0:T(1024)S(1)} %convert_element_type.107, f32[2048]{0:T(1024)S(1)} %add_rsqrt_fusion), kind=kOutput, calls=%fused_computation.73 | convolution fusion | flops 9669967872 | bytes 31993856 | tf_op jit(solution)/shard_map/dot_general | solution.py:62
  247.9 11.3 %all-gather.6.cloned.1.call-done = bf16[2048,1024]{1,0:T(8,128)(2,1)} async-done(((bf16[2048,256]{1,0:T(8,128)(2,1)}), bf16[2048,1024]{1,0:T(8,128)(2,1)}) %all-gather.6.cloned.1.call-update) | async-done | bytes 4194320 | tf_op jit(solution)/shard_map/all_gather | solution.py:74
  259.2 18.2 %multiply_convert_fusion.1 = (bf16[2048,1152]{1,0:T(8,128)(2,1)}, bf16[2048,1152]{1,0:T(8,128)(2,1)}, bf16[2048,1152]{1,0:T(8,128)(2,1)}) fusion(f32[2048,2304]{1,0:T(8,128)} %fusion.33, bf16[2048,1024]{1,0:T(8,128)(2,1)} %all-gather.6.cloned.1.call-done, bf16[1152,1024]{1,0:T(8,128)(2,1)S(1)} %copy-done), kind=kOutput, calls=%fused_computation.5 | convolution fusion | flops 4869586944 | bytes 39583744 | tf_op jit(solution)/shard_map/dot_general | solution.py:75
  277.4 15.8 %fusion.4 = f32[2048,1024]{1,0:T(8,128)} fusion(bf16[1024,2304]{1,0:T(8,128)(2,1)} %bitcast.28, bf16[2048,1152]{1,0:T(8,128)(2,1)} %get-tuple-element.31, bf16[2048,1152]{1,0:T(8,128)(2,1)} %get-tuple-element.30), kind=kOutput, calls=%fused_computation.17 | convolution fusion | flops 9682550784 | bytes 22544384 | tf_op jit(solution)/shard_map/dot_general | solution.py:83
  293.9 9.5 %convolution_convert_fusion.1 = bf16[2048,1024]{1,0:T(8,128)(2,1)} fusion(bf16[2048,1152]{1,0:T(8,128)(2,1)} %get-tuple-element.32, bf16[1152,1024]{1,0:T(8,128)(2,1)S(1)} %copy-done), kind=kOutput, calls=%fused_computation.20 | convolution fusion | flops 4833935360 | bytes 11272192 | tf_op jit(solution)/shard_map/dot_general | solution.py:68
  303.5 142.9 %all-reduce.8.cloned.1.call-done = f32[2048,1024]{1,0:T(8,128)} async-done(((f32[2048,1024]{1,0:T(8,128)}), f32[2048,1024]{1,0:T(8,128)}) %all-reduce.8.cloned.1.call-update) | async-done | bytes 8388624 | tf_op jit(solution)/shard_map/psum | solution.py:84
  446.3 7.1 multiply_reduce_fusion
  453.4 1.4 copy-done.4
  454.9 7.7 multiply_add_fusion
  462.6 2.9 fusion.21
  465.5 1.4 copy-done.2
  466.9 1.4 copy-done.13
  468.2 1.1 multiply_reduce_fusion.5
  469.4 1.3 collective-permute-start.1
  470.7 4.2 collective-permute-done.1
  477.0 0.9 copy-done.16
  477.8 5.0 convolution_convert_fusion.2
  483.0 16.9 %fusion.5 = bf16[1024,2304]{1,0:T(8,128)(2,1)} fusion(bf16[2048,1152]{1,0:T(8,128)(2,1)} %get-tuple-element.31, bf16[2048,1152]{1,0:T(8,128)(2,1)} %get-tuple-element.30, f32[2048,1024]{1,0:T(8,128)} %copy-done.3, f32[1024]{0:T(1024)S(1)} %convert_element_type.107, f32[2048]{0:T(1024)S(1)} %add_rsqrt_fusion), kind=kOutput, calls=%fused_computation.18 | convolution fusion | flops 9691201536 | bytes 22556672 | tf_op jit(solution)/shard_map/dot_general | solution.py:80
  500.0 10.3 %convert_element_type.131 = bf16[1024,2,1152]{2,1,0:T(2,128)(2,1)} reshape(bf16[1024,2304]{1,0:T(8,128)(2,1)} %fusion.5) | data formatting | bytes 9437184 | tf_op jit(solution)/shard_map/convert_element_type | solution.py:136
  510.3 9.6 %convolution_convert_fusion = bf16[1152,1024]{1,0:T(8,128)(2,1)} fusion(bf16[2048,1152]{1,0:T(8,128)(2,1)} %get-tuple-element.32, bf16[2048,1024]{1,0:T(8,128)(2,1)} %all-gather.6.cloned.1.call-done), kind=kOutput, calls=%fused_computation.19 | convolution fusion | flops 4833017856 | bytes 11272192 | tf_op jit(solution)/shard_map/dot_general | solution.py:76
  519.9 5.6 fusion.23
  525.6 4.0 convolution_convert_fusion.3
  529.6 1.6 copy.28
  531.9 3.2 add_convert_fusion
  535.1 5.0 reduce-scatter.5.cloned.1.call-done
  540.1 2.1 fusion.17
  542.2 22.3 %all-reduce = (bf16[256]{0:T(256)(128)(2,1)S(1)}, bf16[3,256]{1,0:T(4,128)(2,1)S(1)}, bf16[256]{0:T(256)(128)(2,1)S(1)}) all-reduce(bf16[256]{0:T(256)(128)(2,1)S(1)} %get-tuple-element.14, bf16[3,256]{1,0:T(4,128)(2,1)S(1)} %pad_maximum_fusion.10, ...), channel_id=1, replica_groups=mesh['dp'=2,'seq'=4,'chan'=4] {'dp','seq'}, use_global_device_ids=true, to_apply=%region_10.0 | all-reduce | flops 1280 | bytes 5120 | tf_op jit(solution)/shard_map/psum | solution.py:131
  566.3 6.1 psum.72
  572.4 3.1 fusion.16
  575.6 262.1 %all-reduce.10.cloned.1.call-done = (bf16[1024,3,256]{2,0,1:T(8,128)(2,1)}, bf16[256,1024]{1,0:T(8,128)(2,1)}, bf16[1024,2,1152]{2,1,0:T(2,128)(2,1)}, bf16[1152,1024]{1,0:T(8,128)(2,1)}) async-done(((bf16[1024,3,256]{2,0,1:T(8,128)(2,1)}, bf16[256,1024]{1,0:T(8,128)(2,1)}, bf16[1024,2,1152]{2,1,0:T(2,128)(2,1)}, bf16[1152,1024]{1,0:T(8,128)(2,1)}), (bf16[1024,3,256]{2,0,1:T(8,128)(2,1)}, ...) | async-done | bytes 9175056 | tf_op jit(solution)/shard_map/psum | solution.py:132
  837.7 7.3 convert_element_type.132
  845.0 2.9 convert_element_type.134
  848.0 1.9 convert_element_type.124
  849.9 1.1 convert_element_type.127
  (98 shorter events, 8.0 us)
Async XLA Ops:
  7.2 252.0 %copy-start = (bf16[1152,1024]{1,0:T(8,128)(2,1)S(1)}, bf16[1152,1024]{1,0:T(8,128)(2,1)}, u32[]{:S(2)}) copy-start(bf16[1152,1024]{1,0:T(8,128)(2,1)} %param.16) | copy-start | bytes 7077892
  7.2 3.4 copy-start.29
  7.2 40.1 %all-gather.4.cloned.1.call-start = ((), (), s32[]{:S(2)}) async-start(), calls=%async_computation.2 | async-start | bytes 5242880 | tf_op jit(solution)/shard_map/all_gather | solution.py:37
  7.9 214.5 %all-reduce.6.cloned.1.call-start = ((), (), s32[]{:S(2)}) async-start(), calls=%async_computation.3 | async-start | bytes 16777216 | tf_op jit(solution)/shard_map/psum | solution.py:57
  16.6 39.2 %copy-start.26 = (f32[4,1,256]{2,1,0:T(1,128)}, f32[4,1,256]{2,1,0:T(1,128)S(1)}, u32[]{:S(2)}) copy-start(f32[4,1,256]{2,1,0:T(1,128)S(1)} %convert_element_type.135) | copy-start | bytes 12292
  47.3 3.4 copy-start.8
  50.6 5.2 copy-start.23
  55.8 7.2 copy-start.5
  55.8 3.9 copy-start.25
  56.1 6.9 copy-start.6
  56.1 7.9 copy-start.15
  56.1 4.8 collective-permute-start
  63.0 1.0 copy-start.10
  68.6 1.1 copy-start.28
  68.7 190.5 %all-gather.6.cloned.1.call-start = ((), (), s32[]{:S(2)}) async-start(), calls=%async_computation.5 | async-start | bytes 5242880 | tf_op jit(solution)/shard_map/all_gather | solution.py:74
  69.4 376.9 %all-reduce.8.cloned.1.call-start = ((), (), s32[]{:S(2)}) async-start(), calls=%async_computation.6 | async-start | bytes 16777216 | tf_op jit(solution)/shard_map/psum | solution.py:84
  228.2 3.4 copy-start.3
  293.3 238.6 %reduce-scatter.3.cloned.1.call-start = ((), (), s32[]{:S(2)}) async-start(), calls=%async_computation.4 | async-start | bytes 5242880 | tf_op jit(solution)/shard_map/reduce_scatter | solution.py:67
  303.4 236.7 %reduce-scatter.5.cloned.1.call-start = ((), (), s32[]{:S(2)}) async-start(), calls=%async_computation.7 | async-start | bytes 5242880 | tf_op jit(solution)/shard_map/reduce_scatter | solution.py:117
  446.3 8.5 copy-start.4
  446.3 20.5 %slice-start = ((s8[6291456]{0:T(1024)(128)(4,1)}), s8[4194304]{0:T(1024)(128)(4,1)S(1)}, s32[]{:S(2)}) async-start(s8[6291456]{0:T(1024)(128)(4,1)} %bitcast.24), calls=%async_computation.9 | async-start | bytes 8388608
  454.9 12.0 %slice-start.1 = ((s8[6291456]{0:T(1024)(128)(4,1)}), s8[2097152]{0:T(1024)(128)(4,1)S(1)}, s32[]{:S(2)}) async-start(s8[6291456]{0:T(1024)(128)(4,1)} %bitcast.24), calls=%async_computation.10 | async-start | bytes 4194304
  462.6 4.3 copy-start.2
  462.6 4.3 copy-start.7
  462.6 5.6 copy-start.13
  469.4 5.5 collective-permute-start.1
  475.6 1.0 copy-start.18
  475.6 2.2 copy-start.16
  476.0 1.0 copy-start.20
  482.8 354.9 %all-reduce.10.cloned.1.call-start = ((), (), s32[]{:S(2)}) async-start(), calls=%async_computation.8 | async-start | bytes 18350080 | tf_op jit(solution)/shard_map/psum | solution.py:132
  510.3 9.6 %copy-start.11 = (bf16[2048,256]{1,0:T(8,128)(2,1)S(1)}, bf16[2048,256]{1,0:T(8,128)(2,1)}, u32[]{:S(2)}) copy-start(bf16[2048,256]{1,0:T(8,128)(2,1)} %copy-done.10) | copy-start | bytes 3145732
  519.8 5.7 copy-start.9
  519.9 5.7 copy-start.19
  519.9 5.7 copy-start.21
  519.9 5.7 copy-start.24
  519.9 5.7 copy-start.27
  531.1 0.7 copy-start.30
  531.8 8.3 copy-start.12
  837.7 7.3 copy-start.14
  845.0 3.0 copy-start.17
  845.0 4.9 copy-start.22
  845.0 6.0 copy-start.1
Sparse Core Ops, SparseCore 0:
  9.6 37.7 all-gather.3
  68.8 153.6 all-reduce.5
  224.0 35.1 all-gather.5
  293.4 152.8 all-reduce.7
  448.7 44.5 reduce-scatter.2
  495.7 44.3 reduce-scatter.4
  545.9 291.7 all-reduce.9
where the time goes:
time: 864 us; the launch traced here: 858 us
  waiting for transfers between devices  606 us (70%)
  matrix products  114 us (13%)
  other arithmetic  51.8 us (6%)
  blocking collectives  34.5 us (4%)
  local copies, waits for them, and re-layouts  31.2 us (4%)
  between operations  14.8 us (2%)
    psum x1, waiting for transfers between devices, shards(): lax.psum(grad_in.astype(jnp.bfloat16), ('dp', 'seq')).astype(jnp.float32)  262 us
    psum x1, waiting for transfers between devices, shards(): resid = x_float + lax.psum(mix_partial, 'chan')  147 us
    psum x1, waiting for transfers between devices, shards(): d_norm_two = lax.psum(norm_partial, 'chan')  143 us
    all_gather x1, waiting for transfers between devices, shards(): lax.all_gather(tokens, 'chan', axis=1, tiled=True)  30.7 us
    psum x1, blocking collectives, shards(): lax.psum(grad_gain_one.astype(jnp.bfloat16), ('dp', 'seq'))  22.3 us
    unnamed x69, local copies, waits for them, and re-layouts  19.2 us
    dot_general x1, matrix products, shards(): jnp.dot(cot_full, down_weight.T, preferred_element_type=jnp.float32)  18.2 us
  transfers between devices with their start and end apart: 9, of which 8 were waited for; matrix products, arithmetic and copies ran while one was open for 14% of the time, Pallas kernels for 0%

commit v1 on v0

--- a/solution.py
+++ b/solution.py
@@ -54,7 +54,7 @@
     )
     mixed = (gate_c * conv_out).astype(jnp.bfloat16)
     mix_partial = jnp.dot(mixed, out_weight, preferred_element_type=jnp.float32)
-    resid = x_float + lax.psum(mix_partial, "chan")
+    resid = x_float + jnp.sum(lax.all_gather(mix_partial, "chan"), axis=0)
     inv_two = lax.rsqrt(jnp.mean(resid * resid, axis=-1, keepdims=True) + epsilon)
     scaled_two = resid * inv_two
     normed_two = (scaled_two * gain_second).astype(jnp.bfloat16)

time: 864 us -> 919 us (1.064)
  waiting for transfers between devices: 606 us -> 644 us
  other arithmetic: 51.8 us -> 68.9 us
    all_gather x0 -> x1, waiting for transfers between devices: none -> 196 us  [shards(): resid = x_float + jnp.sum(lax.all_gather(mix_partial, 'chan'), axis=0)]
    psum x1 -> x0, waiting for transfers between devices: 147 us -> none  [shards(): resid = x_float + lax.psum(mix_partial, 'chan')]
    reduce_sum x0 -> x1, other arithmetic: none -> 17.2 us  [shards(): resid = x_float + jnp.sum(lax.all_gather(mix_partial, 'chan'), axis=0)]
    all_gather x1, waiting for transfers between devices: 11.3 us -> 0.01 us  [shards(): cot_full = lax.all_gather(cotangent, 'chan', axis=1, tiled=True)]
    unnamed x69 -> x73, local copies, waits for them, and re-layouts: 19.2 us -> 19.3 us
  transfers between devices with their start and end apart: 9 -> 9, of which waited for: 8 -> 7; matrix products, arithmetic and copies ran while one was open for 14% -> 15% of each run, Pallas kernels for 0% -> 0%
where the time goes in v1:
time: 919 us; the launch traced here: 912 us
  waiting for transfers between devices  644 us (70%)
  matrix products  113 us (12%)
  other arithmetic  68.9 us (7%)
  blocking collectives  34.5 us (4%)
  local copies, waits for them, and re-layouts  31.2 us (3%)
  between operations  14.9 us (2%)
    psum x1, waiting for transfers between devices, shards(): lax.psum(grad_in.astype(jnp.bfloat16), ('dp', 'seq')).astype(jnp.float32)  262 us
    all_gather x1, waiting for transfers between devices, shards(): resid = x_float + jnp.sum(lax.all_gather(mix_partial, 'chan'), axis=0)  196 us
    psum x1, waiting for transfers between devices, shards(): d_norm_two = lax.psum(norm_partial, 'chan')  143 us
    all_gather x1, waiting for transfers between devices, shards(): lax.all_gather(tokens, 'chan', axis=1, tiled=True)  30.7 us
    psum x1, blocking collectives, shards(): lax.psum(grad_gain_one.astype(jnp.bfloat16), ('dp', 'seq'))  22.3 us
    unnamed x73, local copies, waits for them, and re-layouts  19.3 us
  transfers between devices with their start and end apart: 9, of which 7 were waited for; matrix products, arithmetic and copies ran while one was open for 15% of the time, Pallas kernels for 0%

profile of v1, /device:TPU:0, one launch (start us, length us, event | category | flops | bytes accessed | tf_op | source)
XLA Modules:
  0.0 912.2 jit_solution(16951768124615259269)
XLA Ops:
  8.0 2.6 copy.25
  10.6 6.0 all-gather.1
  16.6 30.7 %all-gather.6.cloned.1.call-done = bf16[2048,1024]{1,0:T(8,128)(2,1)} async-done(((bf16[2048,256]{1,0:T(8,128)(2,1)}), bf16[2048,1024]{1,0:T(8,128)(2,1)}) %all-gather.6.cloned.1.call-update) | async-done | bytes 4194320 | tf_op jit(solution)/shard_map/all_gather | solution.py:37
  47.3 3.2 fusion
  50.8 5.0 fusion.27
  56.1 3.5 collective-permute-start
  59.7 1.3 collective-permute-done
  61.0 2.0 multiply_convert_fusion.7
  63.0 1.0 copy-done.10
  64.0 4.7 fusion.36
  70.0 5.4 copy.30
  75.4 195.8 %all-gather.10.cloned.1.call-done = f32[8192,1024]{1,0:T(8,128)} async-done(((f32[2048,1024]{1,0:T(8,128)}), f32[8192,1024]{1,0:T(8,128)}) %all-gather.10.cloned.1.call-update) | async-done | bytes 33554448 | tf_op jit(solution)/shard_map/all_gather | solution.py:57
  271.2 17.2 %reduce_sum.91 = f32[2048,1024]{1,0:T(8,128)} reduce(f32[4,2048,1024]{2,1,0:T(8,128)} %bitcast.25, f32[]{:T(128)} %constant.8.clone.1), dimensions={0}, to_apply=%region_1.0 | reduce | flops 6291456 | bytes 41943044 | tf_op jit(solution)/shard_map/reduce_sum | solution.py:57
  288.4 5.7 multiply_reduce_fusion.2
  294.2 3.4 copy-done.3
  297.5 15.7 %fusion.33 = f32[2048,2304]{1,0:T(8,128)} fusion(bf16[1024,2304]{1,0:T(8,128)(2,1)} %bitcast.29, f32[2048,1024]{1,0:T(8,128)S(1)} %get-tuple-element.27, f32[1024]{0:T(1024)S(1)} %convert_element_type.107, f32[2048]{0:T(1024)S(1)} %add_rsqrt_fusion), kind=kOutput, calls=%fused_computation.73 | convolution fusion | flops 9669967872 | bytes 31993856 | tf_op jit(solution)/shard_map/dot_general | solution.py:62
  313.3 18.2 %multiply_convert_fusion.1 = (bf16[2048,1152]{1,0:T(8,128)(2,1)}, bf16[2048,1152]{1,0:T(8,128)(2,1)}, bf16[2048,1152]{1,0:T(8,128)(2,1)}) fusion(f32[2048,2304]{1,0:T(8,128)} %fusion.33, bf16[2048,1024]{1,0:T(8,128)(2,1)} %all-gather.8.cloned.1.call-done, bf16[1152,1024]{1,0:T(8,128)(2,1)S(1)} %copy-done), kind=kOutput, calls=%fused_computation.5 | convolution fusion | flops 4869586944 | bytes 39583744 | tf_op jit(solution)/shard_map/dot_general | solution.py:75
  331.5 15.9 %fusion.4 = f32[2048,1024]{1,0:T(8,128)} fusion(bf16[1024,2304]{1,0:T(8,128)(2,1)} %bitcast.30, bf16[2048,1152]{1,0:T(8,128)(2,1)} %get-tuple-element.31, bf16[2048,1152]{1,0:T(8,128)(2,1)} %get-tuple-element.30), kind=kOutput, calls=%fused_computation.17 | convolution fusion | flops 9682550784 | bytes 22544384 | tf_op jit(solution)/shard_map/dot_general | solution.py:83
  347.6 9.5 %convolution_convert_fusion.1 = bf16[2048,1024]{1,0:T(8,128)(2,1)} fusion(bf16[2048,1152]{1,0:T(8,128)(2,1)} %get-tuple-element.32, bf16[1152,1024]{1,0:T(8,128)(2,1)S(1)} %copy-done), kind=kOutput, calls=%fused_computation.20 | convolution fusion | flops 4833935360 | bytes 11272192 | tf_op jit(solution)/shard_map/dot_general | solution.py:68
  357.2 143.3 %all-reduce.5.cloned.1.call-done = f32[2048,1024]{1,0:T(8,128)} async-done(((f32[2048,1024]{1,0:T(8,128)}), f32[2048,1024]{1,0:T(8,128)}) %all-reduce.5.cloned.1.call-update) | async-done | bytes 8388624 | tf_op jit(solution)/shard_map/psum | solution.py:84
  500.5 7.1 multiply_reduce_fusion
  507.6 1.4 copy-done.4
  509.0 7.7 multiply_add_fusion
  516.7 2.9 fusion.21
  519.6 1.4 copy-done.2
  521.0 1.4 copy-done.13
  522.4 1.1 multiply_reduce_fusion.5
  523.4 1.3 collective-permute-start.1
  524.7 4.2 collective-permute-done.1
  531.1 0.9 copy-done.16
  531.9 4.9 convolution_convert_fusion.2
  537.1 16.9 %fusion.5 = bf16[1024,2304]{1,0:T(8,128)(2,1)} fusion(bf16[2048,1152]{1,0:T(8,128)(2,1)} %get-tuple-element.31, bf16[2048,1152]{1,0:T(8,128)(2,1)} %get-tuple-element.30, f32[2048,1024]{1,0:T(8,128)} %copy-done.3, f32[1024]{0:T(1024)S(1)} %convert_element_type.107, f32[2048]{0:T(1024)S(1)} %add_rsqrt_fusion), kind=kOutput, calls=%fused_computation.18 | convolution fusion | flops 9691201536 | bytes 22556672 | tf_op jit(solution)/shard_map/dot_general | solution.py:80
  554.1 10.3 %convert_element_type.131 = bf16[1024,2,1152]{2,1,0:T(2,128)(2,1)} reshape(bf16[1024,2304]{1,0:T(8,128)(2,1)} %fusion.5) | data formatting | bytes 9437184 | tf_op jit(solution)/shard_map/convert_element_type | solution.py:136
  564.4 9.6 %convolution_convert_fusion = bf16[1152,1024]{1,0:T(8,128)(2,1)} fusion(bf16[2048,1152]{1,0:T(8,128)(2,1)} %get-tuple-element.32, bf16[2048,1024]{1,0:T(8,128)(2,1)} %all-gather.8.cloned.1.call-done), kind=kOutput, calls=%fused_computation.19 | convolution fusion | flops 4833017856 | bytes 11272192 | tf_op jit(solution)/shard_map/dot_general | solution.py:76
  574.1 5.6 fusion.23
  579.7 4.0 convolution_convert_fusion.3
  583.7 1.6 copy.28
  586.1 3.2 add_convert_fusion
  589.3 5.0 reduce-scatter.5.cloned.1.call-done
  594.3 2.1 fusion.17
  596.4 22.3 %all-reduce = (bf16[256]{0:T(256)(128)(2,1)S(1)}, bf16[3,256]{1,0:T(4,128)(2,1)S(1)}, bf16[256]{0:T(256)(128)(2,1)S(1)}) all-reduce(bf16[256]{0:T(256)(128)(2,1)S(1)} %get-tuple-element.14, bf16[3,256]{1,0:T(4,128)(2,1)S(1)} %pad_maximum_fusion.10, ...), channel_id=1, replica_groups=mesh['dp'=2,'seq'=4,'chan'=4] {'dp','seq'}, use_global_device_ids=true, to_apply=%region_10.0 | all-reduce | flops 1280 | bytes 5120 | tf_op jit(solution)/shard_map/psum | solution.py:131
  620.4 6.1 psum.64
  626.6 3.1 fusion.16
  629.7 262.1 %all-reduce.7.cloned.1.call-done = (bf16[1024,3,256]{2,0,1:T(8,128)(2,1)}, bf16[256,1024]{1,0:T(8,128)(2,1)}, bf16[1024,2,1152]{2,1,0:T(2,128)(2,1)}, bf16[1152,1024]{1,0:T(8,128)(2,1)}) async-done(((bf16[1024,3,256]{2,0,1:T(8,128)(2,1)}, bf16[256,1024]{1,0:T(8,128)(2,1)}, bf16[1024,2,1152]{2,1,0:T(2,128)(2,1)}, bf16[1152,1024]{1,0:T(8,128)(2,1)}), (bf16[1024,3,256]{2,0,1:T(8,128)(2,1)}, ...) | async-done | bytes 9175056 | tf_op jit(solution)/shard_map/psum | solution.py:132
  891.9 7.3 convert_element_type.132
  899.2 2.9 convert_element_type.134
  902.1 1.9 convert_element_type.124
  904.0 1.1 convert_element_type.127
  (103 shorter events, 7.9 us)
Async XLA Ops:
  7.2 306.1 %copy-start = (bf16[1152,1024]{1,0:T(8,128)(2,1)S(1)}, bf16[1152,1024]{1,0:T(8,128)(2,1)}, u32[]{:S(2)}) copy-start(bf16[1152,1024]{1,0:T(8,128)(2,1)} %param.16) | copy-start | bytes 7077892
  7.2 3.4 copy-start.31
  7.2 40.1 %all-gather.6.cloned.1.call-start = ((), (), s32[]{:S(2)}) async-start(), calls=%async_computation.2 | async-start | bytes 5242880 | tf_op jit(solution)/shard_map/all_gather | solution.py:37
  7.9 263.2 %all-gather.10.cloned.1.call-start = ((), (), s32[]{:S(2)}) async-start(), calls=%async_computation.7 | async-start | bytes 41943040 | tf_op jit(solution)/shard_map/all_gather | solution.py:57
  16.6 39.2 %copy-start.28 = (f32[4,1,256]{2,1,0:T(1,128)}, f32[4,1,256]{2,1,0:T(1,128)S(1)}, u32[]{:S(2)}) copy-start(f32[4,1,256]{2,1,0:T(1,128)S(1)} %convert_element_type.135) | copy-start | bytes 12292
  47.3 3.4 copy-start.8
  50.6 5.2 copy-start.25
  55.8 7.2 copy-start.5
  55.8 3.9 copy-start.27
  56.1 6.9 copy-start.6
  56.1 7.9 copy-start.15
  56.1 4.8 collective-permute-start
  63.0 1.0 copy-start.10
  68.7 1.3 copy-start.30
  68.7 244.6 %all-gather.8.cloned.1.call-start = ((), (), s32[]{:S(2)}) async-start(), calls=%async_computation.4 | async-start | bytes 5242880 | tf_op jit(solution)/shard_map/all_gather | solution.py:74
  69.5 431.0 %all-reduce.5.cloned.1.call-start = ((), (), s32[]{:S(2)}) async-start(), calls=%async_computation.5 | async-start | bytes 16777216 | tf_op jit(solution)/shard_map/psum | solution.py:84
  294.1 3.4 copy-start.3
  347.4 238.7 %reduce-scatter.3.cloned.1.call-start = ((), (), s32[]{:S(2)}) async-start(), calls=%async_computation.3 | async-start | bytes 5242880 | tf_op jit(solution)/shard_map/reduce_scatter | solution.py:67
  357.2 237.1 %reduce-scatter.5.cloned.1.call-start = ((), (), s32[]{:S(2)}) async-start(), calls=%async_computation.6 | async-start | bytes 5242880 | tf_op jit(solution)/shard_map/reduce_scatter | solution.py:117
  500.5 8.5 copy-start.4
  500.5 20.5 %slice-start = ((s8[6291456]{0:T(1024)(128)(4,1)}), s8[4194304]{0:T(1024)(128)(4,1)S(1)}, s32[]{:S(2)}) async-start(s8[6291456]{0:T(1024)(128)(4,1)} %bitcast.26), calls=%async_computation.9 | async-start | bytes 8388608
  509.0 12.0 %slice-start.1 = ((s8[6291456]{0:T(1024)(128)(4,1)}), s8[2097152]{0:T(1024)(128)(4,1)S(1)}, s32[]{:S(2)}) async-start(s8[6291456]{0:T(1024)(128)(4,1)} %bitcast.26), calls=%async_computation.10 | async-start | bytes 4194304
  516.7 4.3 copy-start.2
  516.7 4.3 copy-start.7
  516.7 5.6 copy-start.13
  523.4 6.7 copy-start.18
  523.4 5.5 collective-permute-start.1
  529.7 1.0 copy-start.20
  529.7 2.2 copy-start.16
  530.1 1.0 copy-start.22
  536.9 355.0 %all-reduce.7.cloned.1.call-start = ((), (), s32[]{:S(2)}) async-start(), calls=%async_computation.8 | async-start | bytes 18350080 | tf_op jit(solution)/shard_map/psum | solution.py:132
  564.4 9.6 %copy-start.11 = (bf16[2048,256]{1,0:T(8,128)(2,1)S(1)}, bf16[2048,256]{1,0:T(8,128)(2,1)}, u32[]{:S(2)}) copy-start(bf16[2048,256]{1,0:T(8,128)(2,1)} %copy-done.10) | copy-start | bytes 3145732
  574.0 5.7 copy-start.9
  574.0 5.7 copy-start.19
  574.0 5.7 copy-start.21
  574.0 5.7 copy-start.23
  574.0 5.7 copy-start.26
  574.0 5.7 copy-start.29
  585.3 0.7 copy-start.32
  585.9 8.3 copy-start.12
  891.9 7.3 copy-start.14
  899.1 3.0 copy-start.17
  899.2 4.9 copy-start.24
  899.2 6.0 copy-start.1
Sparse Core Ops, SparseCore 0:
  9.6 37.7 all-gather.5
  68.8 202.2 all-gather.9
  272.7 34.9 all-gather.7
  347.5 152.9 all-reduce.4
  502.9 44.5 reduce-scatter.2
  549.8 44.3 reduce-scatter.4
  600.0 291.7 all-reduce.6
